TPU v7x, 32 devices: a whole 2x2x4 slice. The times are simulated.
32 devices in a mesh: dp: 16 (over z, y, core), tensor: 2 (over x).
Axes of the slice: x: 2, y: 2, z: 4, core: 2. Of those that a mesh axis runs over, the one named last changes fastest.
Arguments:
- inputs: bfloat16 [9216, 8192], P('dp', 'tensor'), may hold values from -6 to 6
- out_grads: bfloat16 [9216, 11264], P('dp', 'tensor'), may hold values from -600 to 600
- basis: bfloat16 [8192, 512], P('dp', 'tensor'), may hold values from -40 to 40
- weight: bfloat16 [8192, 11264], P('dp', 'tensor'), may hold values from -0.099609375 to 0.099609375
- first_moment: float32 [512, 11264], P('dp', 'tensor'), may hold values from -0.9 to 0.9
- second_moment: float32 [512, 11264], P('dp', 'tensor'), may hold values from 0.01 to 1
Outputs:
- new_weight: bfloat16 [8192, 11264], P('dp', 'tensor')
- new_first: float32 [512, 11264], P('dp', 'tensor')
- new_second: float32 [512, 11264], P('dp', 'tensor')
All inputs are finite; a program needn't handle non-finite values.
Results may differ from a plain program's by a relative error of at most 0.0087.
Values may be sent and summed in bfloat16 or wider, within the bound.
A program may use at most 64 MiB of HBM per device.

v0:
```python
import math

import jax
import jax.numpy as jnp
from jax import lax
from jax.sharding import PartitionSpec as P

FW = 11264
R = 512


beta_one = 0.9
beta_two = 0.999
adam_eps = 1e-08
corr_one = 1.0 - 0.9**10
corr_two = 1.0 - 0.999**10
step_size = 0.002
decay_keep = 0.99


def adam_update(lowrank, square, first_moment, second_moment):
    bound_norm = math.sqrt(R * FW)
    factor = jnp.minimum(1.0, bound_norm / (jnp.sqrt(square) + 1e-06))
    clipped = lowrank * factor
    first = beta_one * first_moment + (1.0 - beta_one) * clipped
    second = beta_two * second_moment + (1.0 - beta_two) * clipped * clipped
    update = (first / corr_one / (jnp.sqrt(second / corr_two) + adam_eps)).astype(jnp.bfloat16)
    return (first, second, update)


def on_device(inputs, out_grads, basis, weight, first_moment, second_moment):
    columns = lax.all_gather(basis, "dp", axis=0, tiled=True)
    regrouped = lax.all_to_all(columns, "tensor", split_axis=0, concat_axis=1, tiled=True)
    partial_value = jnp.dot(inputs, regrouped, preferred_element_type=jnp.float32)
    projected = lax.psum(partial_value, "tensor").astype(jnp.bfloat16)
    partial_low = lax.dot_general(
        projected, out_grads, (((0,), (0,)), ((), ())), preferred_element_type=jnp.float32
    )
    own_rows = lax.psum_scatter(partial_low, "dp", scatter_dimension=0, tiled=True)
    square = lax.psum(jnp.sum(own_rows * own_rows), ("dp", "tensor"))
    first, second, update = adam_update(own_rows, square, first_moment, second_moment)
    back_basis = lax.all_gather(basis, "tensor", axis=1, tiled=True)
    delta = jnp.dot(
        back_basis,
        lax.all_gather(update, "dp", axis=0, tiled=True),
        preferred_element_type=jnp.float32,
    )
    new_weight = (decay_keep * weight.astype(jnp.float32) - step_size * delta).astype(jnp.bfloat16)
    return (new_weight, first, second)


def solution(mesh):
    placed = (
        P("dp", "tensor"),
        P("dp", "tensor"),
        P("dp", "tensor"),
        P("dp", "tensor"),
        P("dp", "tensor"),
        P("dp", "tensor"),
    )
    return jax.shard_map(
        on_device,
        mesh=mesh,
        in_specs=placed,
        out_specs=(P("dp", "tensor"), P("dp", "tensor"), P("dp", "tensor")),
        check_vma=False,
    )
```

profile of v0, /device:TPU:0, one launch (start us, length us, event | category | flops | bytes accessed | tf_op | source)
XLA Modules:
  0.0 424.6 jit_solution(6178507596660154082)
XLA Ops:
  7.2 0.0 all-gather.3.cloned.1.call-start
  7.2 0.7 all-gather.3.cloned.1.call-update
  7.9 0.0 reduce-scatter.2.cloned.1.call-start
  7.9 55.3 %all-gather.3.cloned.1.call-done = bf16[8192,256]{1,0:T(8,128)(2,1)} async-done(((bf16[512,256]{1,0:T(8,128)(2,1)}), bf16[8192,256]{1,0:T(8,128)(2,1)}) %all-gather.3.cloned.1.call-update) | async-done | bytes 4194320 | tf_op jit(solution)/shard_map/all_gather | solution.py:32
  63.3 55.5 %all_to_all.19 = bf16[2,4096,256]{2,1,0:T(8,128)(2,1)} all-to-all(bf16[2,4096,256]{2,1,0:T(8,128)(2,1)} %bitcast.14), channel_id=1, replica_groups=mesh['dp'=16,'tensor'=2] {'tensor'}, dimensions={0} | all-to-all | bytes 8388608 | tf_op jit(solution)/shard_map/all_to_all | solution.py:33
  118.7 6.3 %copy.14 = bf16[4096,2,256]{0,2,1:T(8,128)(2,1)} copy(bf16[4096,2,256]{2,0,1:T(8,128)(2,1)} %bitcast.13) | data formatting | bytes 8388608 | tf_op jit(solution)/shard_map/all_to_all | solution.py:33
  125.0 5.9 %fusion.5 = f32[576,512]{1,0:T(8,128)S(1)} fusion(bf16[576,4096]{1,0:T(8,128)(2,1)} %param.6, bf16[4096,512]{0,1:T(8,128)(2,1)} %bitcast.15), kind=kOutput, calls=%fused_computation.9 | convolution fusion | flops 2415919104 | bytes 10092544 | tf_op jit(solution)/shard_map/dot_general | solution.py:34
  131.0 30.4 %all-reduce.1 = bf16[576,512]{1,0:T(8,128)(2,1)S(1)} all-reduce(f32[576,512]{1,0:T(8,128)S(1)} %fusion.5), channel_id=1, replica_groups=mesh['dp'=16,'tensor'=2] {'tensor'}, use_global_device_ids=true, to_apply=%region_0.0 | all-reduce | flops 294912 | bytes 1769472 | tf_op jit(solution)/shard_map/psum | solution.py:35
  161.4 10.3 %fusion.6 = f32[512,5632]{1,0:T(8,128)} fusion(bf16[576,512]{1,0:T(8,128)(2,1)S(1)} %all-reduce.1, bf16[576,5632]{1,0:T(8,128)(2,1)} %param.7), kind=kOutput, calls=%fused_computation.10 | convolution fusion | flops 3321888768 | bytes 18612224 | tf_op jit(solution)/shard_map/dot_general | solution.py:36
  171.7 0.0 copy-start.1
  171.7 0.0 copy-start.2
  171.7 0.0 reduce-scatter.2.cloned.1.call-update
  171.8 0.0 all-gather.5.cloned.1.call-start
  171.8 125.4 %reduce-scatter.2.cloned.1.call-done = f32[32,5632]{1,0:T(8,128)} async-done(((f32[512,5632]{1,0:T(8,128)}), f32[32,5632]{1,0:T(8,128)}) %reduce-scatter.2.cloned.1.call-update) | async-done | bytes 720912 | tf_op jit(solution)/shard_map/reduce_scatter | solution.py:39
  297.2 1.9 multiply_reduce_fusion
  299.1 39.9 %psum.15 = f32[]{:T(128)} all-reduce(f32[]{:T(128)} %multiply_reduce_fusion), channel_id=1, replica_groups=mesh['dp'=16,'tensor'=2] {'dp','tensor'}, use_global_device_ids=true, to_apply=%region_3.0 | all-reduce | flops 1 | bytes 8 | tf_op jit(solution)/shard_map/psum | solution.py:40
  339.7 0.0 copy-done.1
  339.8 0.0 copy-done.2
  339.8 2.6 divide_convert_fusion
  342.4 0.0 all-gather.5.cloned.1.call-update
  342.4 0.0 copy-start
  342.4 8.4 %copy.13 = bf16[512,5632]{0,1:T(8,128)(2,1)} copy(bf16[512,5632]{1,0:T(8,128)(2,1)} %param.9) | data formatting | bytes 11534336 | tf_op args[3]
  350.8 0.0 copy-done
  350.8 8.0 %all_gather.11 = bf16[512,512]{1,0:T(8,128)(2,1)S(1)} all-gather(bf16[512,256]{1,0:T(8,128)(2,1)S(1)} %copy-done), channel_id=1, replica_groups=mesh['dp'=16,'tensor'=2] {'tensor'}, dimensions={1}, use_global_device_ids=true | all-gather | bytes 786432 | tf_op jit(solution)/shard_map/all_gather | solution.py:42
  358.8 42.2 %all-gather.5.cloned.1.call-done = bf16[512,5632]{1,0:T(8,128)(2,1)} async-done(((bf16[32,5632]{1,0:T(8,128)(2,1)}), bf16[512,5632]{1,0:T(8,128)(2,1)}) %all-gather.5.cloned.1.call-update) | async-done | bytes 5767184 | tf_op jit(solution)/shard_map/all_gather | solution.py:45
  401.0 8.7 %fusion = bf16[512,5632]{0,1:T(8,128)(2,1)} fusion(bf16[512,5632]{0,1:T(8,128)(2,1)} %copy.13, bf16[512,5632]{1,0:T(8,128)(2,1)} %all-gather.5.cloned.1.call-done, bf16[512,512]{1,0:T(8,128)(2,1)S(1)} %all_gather.11), kind=kOutput, calls=%fused_computation.1 | convolution fusion | flops 2967207936 | bytes 17825792 | tf_op jit(solution)/shard_map/dot_general | solution.py:43
  409.7 8.4 %copy.15 = bf16[512,5632]{1,0:T(8,128)(2,1)} copy(bf16[512,5632]{0,1:T(8,128)(2,1)} %fusion) | data formatting | bytes 11534336
Async XLA Ops:
  7.2 56.1 %all-gather.3.cloned.1.call-start = ((), (), s32[]{:S(2)}) async-start(), calls=%async_computation.2 | async-start | bytes 4456448 | tf_op jit(solution)/shard_map/all_gather | solution.py:32
  7.9 289.3 %reduce-scatter.2.cloned.1.call-start = ((), (), s32[]{:S(2)}) async-start(), calls=%async_computation.3 | async-start | bytes 12255232 | tf_op jit(solution)/shard_map/reduce_scatter | solution.py:39
  171.7 168.0 %copy-start.1 = (f32[32,5632]{1,0:T(8,128)S(1)}, f32[32,5632]{1,0:T(8,128)}, u32[]{:S(2)}) copy-start(f32[32,5632]{1,0:T(8,128)} %param.10) | copy-start | bytes 2162692
  171.7 168.0 %copy-start.2 = (f32[32,5632]{1,0:T(8,128)S(1)}, f32[32,5632]{1,0:T(8,128)}, u32[]{:S(2)}) copy-start(f32[32,5632]{1,0:T(8,128)} %param.11) | copy-start | bytes 2162692
  171.8 229.3 %all-gather.5.cloned.1.call-start = ((), (), s32[]{:S(2)}) async-start(), calls=%async_computation.4 | async-start | bytes 6127616 | tf_op jit(solution)/shard_map/all_gather | solution.py:45
  342.4 8.4 %copy-start = (bf16[512,256]{1,0:T(8,128)(2,1)S(1)}, bf16[512,256]{1,0:T(8,128)(2,1)}, u32[]{:S(2)}) copy-start(bf16[512,256]{1,0:T(8,128)(2,1)} %param.8) | copy-start | bytes 786436
Sparse Core Ops, SparseCore 0:
  10.1 53.0 all-gather.2
  171.9 125.2 reduce-scatter.1
  342.5 58.4 all-gather.4
where the time goes:
time: 426 us; the launch traced here: 425 us
  waiting for transfers between devices  224 us (53%)
  blocking collectives  134 us (31%)
  matrix products  24.9 us (6%)
  local copies, waits for them, and re-layouts  23.1 us (5%)
  between operations  14.5 us (3%)
  other arithmetic  4.48 us (1%)
    reduce_scatter x1, waiting for transfers between devices, on_device(): lax.psum_scatter(partial_low, 'dp', scatter_dimension=0, tiled=True)  125 us
    all_to_all x1, blocking collectives, on_device(): lax.all_to_all(columns, 'tensor', split_axis=0, concat_axis=1, tiled=True)  55.5 us
    all_gather x1, waiting for transfers between devices, on_device(): columns = lax.all_gather(basis, 'dp', axis=0, tiled=True)  55.3 us
    all_gather x1, waiting for transfers between devices, on_device(): lax.all_gather(update, 'dp', axis=0, tiled=True)  42.2 us
    psum x1, blocking collectives, on_device(): square = lax.psum(jnp.sum(own_rows * own_rows), ('dp', 'tensor'))  39.9 us
    psum x1, blocking collectives, on_device(): projected = lax.psum(partial_value, 'tensor').astype(jnp.bfloat16)  30.4 us
    unnamed x8, local copies, waits for them, and re-layouts  16.8 us
    dot_general x1, matrix products, on_device(): lax.dot_general(projected, out_grads, (((0,), (0,)), ((), ())), preferred...  10.3 us
  transfers between devices with their start and end apart: 3, of which 3 were waited for; matrix products, arithmetic and copies ran while one was open for 2% of the time, Pallas kernels for 0%

commit v1 on v0

v1 whole, which is shorter than its diff:
```python
import functools
import math

import jax
import jax.numpy as jnp
from jax import lax
from jax.experimental import pallas as pl
from jax.experimental.pallas import tpu as pltpu
from jax.sharding import PartitionSpec as P

beta_one = 0.9
beta_two = 0.999
adam_eps = 1e-08
corr_one = 1.0 - 0.9**10
corr_two = 1.0 - 0.999**10
step_size = 0.002
decay_keep = 0.99

MESH = pl.DeviceIdType.MESH
ANY = pl.BlockSpec(memory_space=pl.ANY)
VMEM = pl.BlockSpec(memory_space=pltpu.VMEM)


def factors(dp):
    c = 2 if dp % 2 == 0 else 1
    y = 2 if (dp // c) % 2 == 0 else 1
    return dp // (c * y), y, c


def near_first(z):
    return sorted(range(1, z), key=lambda k: (min(k, z - k), k))


class Place:
    def __init__(self, dims, tensor):
        self.dims, self.tensor = dims, tensor
        d = lax.axis_index("dp")
        _, ny, nc = dims
        self.z, self.y, self.c = d // (ny * nc), (d // nc) % ny, d % nc
        self.t = lax.axis_index("tensor")

    def unit(self, k=0, j=0, i=0):
        nz, ny, nc = self.dims
        z = lax.rem(self.z + k + nz, nz) if k else self.z
        y = lax.rem(self.y + j + ny, ny) if j else self.y
        c = lax.rem(self.c + i + nc, nc) if i else self.c
        return (z * ny + y) * nc + c

    def peer(self, k=0, j=0, i=0, s=0):
        t = lax.rem(self.t + s, self.tensor) if s else self.t
        return (self.unit(k, j, i), t)

    def peers(self, tensor=True):
        nz, ny, nc = self.dims
        out = [self.peer(k=k) for k in range(1, nz)]
        out += [self.peer(j=j) for j in range(1, ny)]
        out += [self.peer(i=i) for i in range(1, nc)]
        if tensor:
            out += [self.peer(s=s) for s in range(1, self.tensor)]
        return out


def greet(peers):
    barrier = pltpu.get_barrier_semaphore()
    for p in peers:
        pl.semaphore_signal(barrier, inc=1, device_id=p, device_id_type=MESH)
    pl.semaphore_wait(barrier, len(peers))


def send(src, dst, sems, slot, peer):
    copy = pltpu.make_async_remote_copy(
        src_ref=src,
        dst_ref=dst,
        send_sem=sems.at[0, slot],
        recv_sem=sems.at[1, slot],
        device_id=peer,
        device_id_type=MESH,
    )
    copy.start()
    return copy


def gather(at, own, full, sems, base=0):
    nz, ny, nc = at.dims
    slot = [base]
    pending = []

    def go(k, j, i, src_unit, src):
        copy = send(src, full.at[src_unit], sems, slot[0], at.peer(k, j, i))
        slot[0] += 1
        pending.append(copy)
        return copy

    order = near_first(nz)
    across = {k: go(k, 0, 0, at.unit(), own) for k in order}
    sides, cores = {}, []
    for k in [0] + order:
        if k:
            across[k].wait_recv()
        u = at.unit(-k)
        src = full.at[u] if k else own
        for j in range(1, ny):
            sides[k, j] = go(0, j, 0, u, src)
        for i in range(1, nc):
            cores.append(go(0, 0, i, u, src))
    for k in [0] + order:
        for j in range(1, ny):
            sides[k, j].wait_recv()
            u = at.unit(-k, -j)
            for i in range(1, nc):
                cores.append(go(0, 0, i, u, full.at[u]))
    for copy in cores:
        copy.wait_recv()
    for copy in pending:
        copy.wait_send()


def basis_kernel(dims, tensor, own_ref, back_ref, full, back, sems, local):
    at = Place(dims, tensor)
    dp = math.prod(dims)
    greet(at.peers())
    mine = pltpu.make_async_copy(own_ref, full.at[at.unit()], local.at[0])
    mine_back = pltpu.make_async_copy(back_ref, back.at[at.t], local.at[1])
    mine.start()
    mine_back.start()
    gather(at, own_ref, full, sems)
    backs = [
        send(back_ref, back.at[at.t], sems, dp - 1 + s - 1, at.peer(s=s))
        for s in range(1, tensor)
    ]
    for copy in backs:
        copy.wait()
    mine.wait()
    mine_back.wait()


def gather_basis(moved, basis, dims, tensor):
    dp = math.prod(dims)
    count = dp - 1 + tensor - 1
    return pl.pallas_call(
        functools.partial(basis_kernel, dims, tensor),
        out_shape=(
            jax.ShapeDtypeStruct((dp,) + moved.shape, moved.dtype),
            jax.ShapeDtypeStruct((tensor,) + basis.shape, basis.dtype),
        ),
        in_specs=[ANY, ANY],
        out_specs=(ANY, ANY),
        scratch_shapes=[
            pltpu.SemaphoreType.DMA((2, count)),
            pltpu.SemaphoreType.DMA((2,)),
        ],
        compiler_params=pltpu.CompilerParams(collective_id=0, has_side_effects=True),
        name="gather_basis",
    )(moved, basis)


def project_kernel(tensor, chunks, in_ref, basis_ref, out_ref, own, sent, got, sems):
    me = lax.axis_index("tensor")
    d = lax.axis_index("dp")
    peers = [(d, lax.rem(me + s, tensor)) for s in range(1, tensor)]
    greet(peers)
    tokens = in_ref.shape[0] // chunks
    width = basis_ref.shape[2]
    copies = []
    for a in range(chunks):
        rows = pl.ds(a * tokens, tokens)
        for h in range(tensor):
            part = jnp.dot(in_ref[rows, :], basis_ref[h], preferred_element_type=jnp.float32)
            own[rows, h * width : (h + 1) * width] = part
            sent[rows, h * width : (h + 1) * width] = part.astype(jnp.bfloat16)
        for s in range(1, tensor):
            copies.append(
                send(
                    sent.at[rows],
                    got.at[s - 1, rows],
                    sems,
                    a * (tensor - 1) + s - 1,
                    peers[s - 1],
                )
            )
    for a in range(chunks):
        rows = pl.ds(a * tokens, tokens)
        total = own[rows, :]
        for s in range(1, tensor):
            copies[a * (tensor - 1) + s - 1].wait_recv()
            total = total + got[s - 1, rows, :].astype(jnp.float32)
        out_ref[rows, :] = total.astype(jnp.bfloat16)
    for copy in copies:
        copy.wait_send()


def project(inputs, basis, tensor):
    tokens = inputs.shape[0]
    rank = basis.shape[0] * basis.shape[2]
    chunks = 2
    return pl.pallas_call(
        functools.partial(project_kernel, tensor, chunks),
        out_shape=jax.ShapeDtypeStruct((tokens, rank), jnp.bfloat16),
        in_specs=[VMEM, VMEM],
        out_specs=VMEM,
        scratch_shapes=[
            pltpu.VMEM((tokens, rank), jnp.float32),
            pltpu.VMEM((tokens, rank), jnp.bfloat16),
            pltpu.VMEM((max(tensor - 1, 1), tokens, rank), jnp.bfloat16),
            pltpu.SemaphoreType.DMA((2, chunks * max(tensor - 1, 1))),
        ],
        compiler_params=pltpu.CompilerParams(collective_id=1, has_side_effects=True),
        name="project",
    )(inputs, basis)


def step_kernel(
    dims, tensor, bound_norm, part, m_ref, v_ref,
    first_ref, second_ref, full,
    r1, r2, r3, s1, s2, keep, upd, norm, sems, gather_sems, norm_sems, local,
):
    at = Place(dims, tensor)
    nz, ny, nc = dims
    f32 = jnp.float32
    greet(at.peers())

    order = near_first(nz)[::-1] + [0]
    slot = 0
    first_copies, second_copies, third_copies = {}, {}, {}
    for k in order:
        for j in [*range(1, ny), 0]:
            for i in range(1, nc):
                first_copies[k, j, i] = send(
                    part.at[at.unit(k, j, i)], r1.at[k, j, i - 1], sems, slot, at.peer(i=i)
                )
                slot += 1

    def over_cores(k, j):
        total = part[at.unit(k, j)].astype(f32)
        for i in range(1, nc):
            first_copies[k, j, i].wait_recv()
            total = total + r1[k, j, i - 1].astype(f32)
        return total

    def over_sides(k):
        total = keep[k]
        for j in range(1, ny):
            second_copies[k, j].wait_recv()
            total = total + r2[k, j - 1].astype(f32)
        return total

    def pass_on(k):
        nonlocal slot
        if k == 0:
            return
        s2[k - 1] = over_sides(k).astype(jnp.bfloat16)
        third_copies[k] = send(s2.at[k - 1], r3.at[k - 1], sems, slot, at.peer(k=k))
        slot += 1

    before = None
    for k in order:
        for j in range(1, ny):
            s1[k, j - 1] = over_cores(k, j).astype(jnp.bfloat16)
            second_copies[k, j] = send(s1.at[k, j - 1], r2.at[k, j - 1], sems, slot, at.peer(j=j))
            slot += 1
        keep[k] = over_cores(k, 0)
        if before is not None:
            pass_on(before)
        before = k
    total = over_sides(0)
    for k in order[:-1]:
        third_copies[k].wait_recv()
        total = total + r3[k - 1].astype(f32)
    keep[0] = total

    lanes = norm.shape[-1]
    rows, columns = total.shape
    squares = jnp.sum(total * total, axis=0, keepdims=True)
    folded = squares[:, :lanes]
    for a in range(1, columns // lanes):
        folded = folded + squares[:, a * lanes : (a + 1) * lanes]
    tally = jnp.broadcast_to(folded, (8, lanes))
    norm_copies, place = [], 0
    for count, axis in ((nc, "i"), (ny, "j"), (tensor, "s"), (nz, "k")):
        if count == 1:
            continue
        base = place
        norm[base] = tally
        copies = []
        for step in range(1, count):
            copies.append(
                send(norm.at[base], norm.at[base + step], norm_sems, base + step, at.peer(**{axis: step}))
            )
        for step in range(1, count):
            copies[step - 1].wait_recv()
            tally = tally + norm[base + step]
        norm_copies += copies
        place += count
    square = jnp.sum(tally[0:1, :], axis=1, keepdims=True)

    factor = jnp.minimum(1.0, bound_norm / (jnp.sqrt(square) + 1e-06))
    clipped = keep[0] * factor
    first = beta_one * m_ref[...] + (1.0 - beta_one) * clipped
    second = beta_two * v_ref[...] + (1.0 - beta_two) * clipped * clipped
    first_ref[...] = first
    second_ref[...] = second
    upd[...] = (first / corr_one / (jnp.sqrt(second / corr_two) + adam_eps)).astype(jnp.bfloat16)

    mine = pltpu.make_async_copy(upd, full.at[at.unit()], local)
    mine.start()
    gather(at, upd, full, gather_sems)
    mine.wait()
    for group in (first_copies, second_copies, third_copies):
        for copy in group.values():
            copy.wait_send()
    for copy in norm_copies:
        copy.wait_send()


def reduce_step(part, first_moment, second_moment, dims, tensor, bound_norm):
    dp, rows, columns = part.shape
    nz, ny, nc = dims
    bf16, f32 = jnp.bfloat16, jnp.float32
    sends = nz * ny * (nc - 1) + nz * (ny - 1) + nz - 1
    tallies = sum(n for n in (nz, ny, nc, tensor) if n > 1)
    at_least = lambda n: max(n, 1)
    return pl.pallas_call(
        functools.partial(step_kernel, dims, tensor, bound_norm),
        out_shape=(
            jax.ShapeDtypeStruct((rows, columns), f32),
            jax.ShapeDtypeStruct((rows, columns), f32),
            jax.ShapeDtypeStruct((dp, rows, columns), bf16),
        ),
        in_specs=[VMEM, VMEM, VMEM],
        out_specs=(VMEM, VMEM, ANY),
        scratch_shapes=[
            pltpu.VMEM((nz, ny, at_least(nc - 1), rows, columns), bf16),
            pltpu.VMEM((nz, at_least(ny - 1), rows, columns), bf16),
            pltpu.VMEM((at_least(nz - 1), rows, columns), bf16),
            pltpu.VMEM((nz, at_least(ny - 1), rows, columns), bf16),
            pltpu.VMEM((at_least(nz - 1), rows, columns), bf16),
            pltpu.VMEM((nz, rows, columns), f32),
            pltpu.VMEM((rows, columns), bf16),
            pltpu.VMEM((at_least(tallies), 8, 128), f32),
            pltpu.SemaphoreType.DMA((2, at_least(sends))),
            pltpu.SemaphoreType.DMA((2, dp)),
            pltpu.SemaphoreType.DMA((2, at_least(tallies))),
            pltpu.SemaphoreType.DMA,
        ],
        compiler_params=pltpu.CompilerParams(collective_id=2, has_side_effects=True),
        name="reduce_step",
    )(part, first_moment, second_moment)


def apply_kernel(basis_ref, update_ref, weight_ref, out_ref):
    tensor, _, width = basis_ref.shape
    delta = None
    for s in range(tensor):
        one = jnp.dot(
            basis_ref[s],
            update_ref[s * width : (s + 1) * width, :],
            preferred_element_type=jnp.float32,
        )
        delta = one if delta is None else delta + one
    kept = decay_keep * weight_ref[...].astype(jnp.float32)
    out_ref[...] = (kept - step_size * delta).astype(jnp.bfloat16)


def apply_update(basis, update, weight):
    rows, columns = weight.shape
    rank = update.shape[0]
    blocks = columns // 128
    tile = 128 * max(n for n in range(1, 9) if blocks % n == 0)
    return pl.pallas_call(
        apply_kernel,
        out_shape=jax.ShapeDtypeStruct(weight.shape, weight.dtype),
        grid=(columns // tile,),
        in_specs=[
            pl.BlockSpec(basis.shape, lambda n: (0, 0, 0)),
            pl.BlockSpec((rank, tile), lambda n: (0, n)),
            pl.BlockSpec((rows, tile), lambda n: (0, n)),
        ],
        out_specs=pl.BlockSpec((rows, tile), lambda n: (0, n)),
        name="apply_update",
    )(basis, update, weight)


def on_device(dp, tensor, inputs, out_grads, basis, weight, first_moment, second_moment):
    dims = factors(dp)
    per = dp // tensor
    pairs = []
    for d in range(dp):
        for t in range(tensor):
            target = (t * per + d % per) * tensor + d // per
            pairs.append((d * tensor + t, target))
    moved = lax.ppermute(basis, ("dp", "tensor"), pairs)
    gathered, back = gather_basis(moved, basis, dims, tensor)
    features = inputs.shape[1]
    grouped = gathered.reshape(tensor, features, basis.shape[1])
    projected = project(inputs, grouped, tensor)
    part = lax.dot_general(
        projected, out_grads, (((0,), (0,)), ((), ())), preferred_element_type=jnp.float32
    ).astype(jnp.bfloat16)
    rank, columns = part.shape
    bound_norm = math.sqrt(rank * columns * tensor)
    first, second, update = reduce_step(
        part.reshape(dp, rank // dp, columns), first_moment, second_moment, dims, tensor, bound_norm
    )
    new_weight = apply_update(back, update.reshape(rank, columns), weight)
    return (new_weight, first, second)


def solution(mesh):
    placed = P("dp", "tensor")
    return jax.shard_map(
        functools.partial(on_device, mesh.shape["dp"], mesh.shape["tensor"]),
        mesh=mesh,
        in_specs=(placed,) * 6,
        out_specs=(placed,) * 3,
        check_vma=False,
    )
```

time: 426 us -> 212 us (0.50)
  waiting for transfers between devices: 224 us -> 0.01 us
  Pallas kernels: 0 us -> 197 us
  blocking collectives: 134 us -> 0 us
  local copies, waits for them, and re-layouts: 23.1 us -> 2.43 us
  matrix products: 24.9 us -> 10.3 us
  between operations: 14.5 us -> 0.67 us
  other arithmetic: 4.48 us -> 0 us
    pallas_call x0 -> x4, Pallas kernels: none -> 197 us  [the longest x1 101 us: reduce_step(): pl.pallas_call(functools.partial(step_kernel, dims, tensor, bound_norm),...]
    reduce_scatter x1 -> x0, waiting for transfers between devices: 125 us -> none  [on_device(): lax.psum_scatter(partial_low, 'dp', scatter_dimension=0, tiled=True)]
    all_gather x2 -> x0, waiting for transfers between devices: 97.5 us -> none  [the longest x1 55.3 us: on_device(): columns = lax.all_gather(basis, 'dp', axis=0, tiled=True)]
    psum x2 -> x0, blocking collectives: 70.3 us -> none  [the longest x1 39.9 us: on_device(): square = lax.psum(jnp.sum(own_rows * own_rows), ('dp', 'tensor'))]
    all_to_all x1 -> x0, blocking collectives: 55.5 us -> none  [on_device(): lax.all_to_all(columns, 'tensor', split_axis=0, concat_axis=1, tiled=True)]
    dot_general x2 -> x0, matrix products: 14.6 us -> none  [the longest x1 8.68 us: on_device(): jnp.dot(back_basis, lax.all_gather(update, 'dp', axis=0, tiled=True), pre...]
    unnamed x8, local copies, waits for them, and re-layouts: 16.8 us -> 2.43 us
    all_gather x1 -> x0, blocking collectives: 8.04 us -> none  [on_device(): back_basis = lax.all_gather(basis, 'tensor', axis=1, tiled=True)]
  transfers between devices with their start and end apart: 3 -> 1, of which waited for: 3 -> 0; matrix products, arithmetic and copies ran while one was open for 2% -> 0% of each run, Pallas kernels for 0% -> 0%
where the time goes in v1:
time: 212 us
  Pallas kernels  197 us (93%)
  matrix products  10.3 us (5%)
  local copies, waits for them, and re-layouts  2.43 us (1%)
    pallas_call x1, Pallas kernels, reduce_step(): pl.pallas_call(functools.partial(step_kernel, dims, tensor, bound_norm),...  101 us
    pallas_call x1, Pallas kernels, gather_basis(): pl.pallas_call(functools.partial(basis_kernel, dims, tensor), out_shape=(...  61.6 us
    pallas_call x1, Pallas kernels, project(): pl.pallas_call(functools.partial(project_kernel, tensor, chunks), out_sha...  21.7 us
    pallas_call x1, Pallas kernels, apply_update(): pl.pallas_call(apply_kernel, out_shape=jax.ShapeDtypeStruct(weight.shape,...  12.3 us
    dot_general x1, matrix products, on_device(): lax.dot_general(projected, out_grads, (((0,), (0,)), ((), ())), preferred...  10.3 us
  transfers between devices with their start and end apart: 1, of which 0 were waited for; matrix products, arithmetic and copies ran while one was open for 0% of the time, Pallas kernels for 0%

profile of v1, /device:TPU:0, one launch (start us, length us, event | category | flops | bytes accessed | tf_op | source)
XLA Modules:
  0.0 211.9 jit_solution(4027325430945071930)
XLA Ops:
  0.6 1.6 collective-permute-start
  2.2 0.0 collective-permute-done.own_ref
  2.2 0.0 copy-start.2
  2.2 0.7 copy-done.2
  2.9 61.6 %gather_basis.1 = (bf16[16,512,256]{2,1,0:T(8,128)(2,1)}, bf16[2,512,256]{2,1,0:T(8,128)(2,1)}) custom-call(bf16[512,256]{1,0:T(8,128)(2,1)} %copy-done.2, bf16[512,256]{1,0:T(8,128)(2,1)} %back_ref.1), custom_call_target="tpu_custom_call" | custom-call | tf_op jit(solution)/shard_map/gather_basis/pallas_call | solution.py:140
  64.5 21.7 %project.1 = bf16[576,512]{1,0:T(8,128)(2,1)} custom-call(bf16[576,4096]{1,0:T(8,128)(2,1)} %in_ref.1, bf16[2,4096,256]{2,1,0:T(8,128)(2,1)} %bitcast.7), custom_call_target="tpu_custom_call" | custom-call | tf_op jit(solution)/shard_map/project/pallas_call | solution.py:196
  86.3 10.3 %convolution_convert_fusion = bf16[512,5632]{1,0:T(8,128)(2,1)} fusion(bf16[576,512]{1,0:T(8,128)(2,1)} %project.1, bf16[576,5632]{1,0:T(8,128)(2,1)} %param.7), kind=kOutput, calls=%fused_computation | convolution fusion | flops 3324772352 | bytes 12845056 | tf_op jit(solution)/shard_map/dot_general | solution.py:396
  96.5 101.3 %reduce_step.1 = (f32[32,5632]{1,0:T(8,128)}, f32[32,5632]{1,0:T(8,128)}, bf16[16,32,5632]{2,1,0:T(8,128)(2,1)}) custom-call(bf16[16,32,5632]{2,1,0:T(8,128)(2,1)} %bitcast.6, f32[32,5632]{1,0:T(8,128)} %m_ref.1, f32[32,5632]{1,0:T(8,128)} %v_ref.1), custom_call_target="tpu_custom_call" | custom-call | tf_op jit(solution)/shard_map/reduce_step/pallas_call | solution.py:322
  197.9 0.0 copy-start.1
  197.9 0.0 copy-start
  197.9 12.3 %apply_update.1 = bf16[512,5632]{1,0:T(8,128)(2,1)} custom-call(bf16[2,512,256]{2,1,0:T(8,128)(2,1)} %get-tuple-element.8.basis_ref, bf16[512,5632]{1,0:T(8,128)(2,1)} %bitcast.5, bf16[512,5632]{1,0:T(8,128)(2,1)} %weight_ref.1), custom_call_target="tpu_custom_call" | custom-call | tf_op jit(solution)/shard_map/apply_update/pallas_call | solution.py:369
  210.2 0.0 copy-done.1
  210.2 0.9 copy.11
  211.0 0.0 copy-done
  211.0 0.9 copy.12
Async XLA Ops:
  0.6 1.6 collective-permute-start
  2.2 0.7 copy-start.2
  197.9 12.3 %copy-start.1 = (f32[32,5632]{1,0:T(8,128)S(1)}, f32[32,5632]{1,0:T(8,128)}, u32[]{:S(2)}) copy-start(f32[32,5632]{1,0:T(8,128)} %get-tuple-element.17) | copy-start | bytes 2162692
  197.9 13.1 %copy-start = (f32[32,5632]{1,0:T(8,128)S(1)}, f32[32,5632]{1,0:T(8,128)}, u32[]{:S(2)}) copy-start(f32[32,5632]{1,0:T(8,128)} %get-tuple-element.18) | copy-start | bytes 2162692

commit v2 on v1

v2 whole, which is shorter than its diff:
```python
import functools
import math

import jax
import jax.numpy as jnp
from jax import lax
from jax.experimental import pallas as pl
from jax.experimental.pallas import tpu as pltpu
from jax.sharding import PartitionSpec as P

beta_one = 0.9
beta_two = 0.999
adam_eps = 1e-08
corr_one = 1.0 - 0.9**10
corr_two = 1.0 - 0.999**10
step_size = 0.002
decay_keep = 0.99

MESH = pl.DeviceIdType.MESH
ANY = pl.BlockSpec(memory_space=pl.ANY)
VMEM = pl.BlockSpec(memory_space=pltpu.VMEM)


def factors(dp):
    c = 2 if dp % 2 == 0 else 1
    y = 2 if (dp // c) % 2 == 0 else 1
    return dp // (c * y), y, c


class Place:
    def __init__(self, dims, tensor):
        self.dims, self.tensor = dims, tensor
        self.d = lax.axis_index("dp")
        _, ny, nc = dims
        self.z, self.y, self.c = self.d // (ny * nc), (self.d // nc) % ny, self.d % nc
        self.t = lax.axis_index("tensor")

    def unit(self, z, j=0, i=0):
        _, ny, nc = self.dims
        y = lax.rem(self.y + j + ny, ny) if j else self.y
        c = lax.rem(self.c + i + nc, nc) if i else self.c
        return (z * ny + y) * nc + c

    def peer(self, k=0, j=0, i=0, s=0):
        nz = self.dims[0]
        z = lax.rem(self.z + k + nz, nz) if k else self.z
        t = lax.rem(self.t + s, self.tensor) if s else self.t
        return (self.unit(z, j, i), t)

    def has(self, z):
        return jnp.logical_and(z >= 0, z < self.dims[0])

    def peers(self):
        nz, ny, nc = self.dims
        out = [self.peer(k=k) for k in range(1, nz)]
        out += [self.peer(j=j) for j in range(1, ny)]
        out += [self.peer(i=i) for i in range(1, nc)]
        out += [self.peer(s=s) for s in range(1, self.tensor)]
        return out


def greet(peers, extra=None):
    barrier = pltpu.get_barrier_semaphore()
    for p in peers:
        pl.semaphore_signal(barrier, inc=1, device_id=p, device_id_type=MESH)
    if extra is None:
        pl.semaphore_wait(barrier, len(peers))
        return

    @pl.when(extra[0])
    def _():
        pl.semaphore_signal(barrier, inc=1, device_id=extra[1], device_id_type=MESH)
        pl.semaphore_wait(barrier, len(peers) + 1)

    @pl.when(jnp.logical_not(extra[0]))
    def _():
        pl.semaphore_wait(barrier, len(peers))


def remote(src, dst, sems, slot, peer):
    return pltpu.make_async_remote_copy(
        src_ref=src,
        dst_ref=dst,
        send_sem=sems.at[0, slot],
        recv_sem=sems.at[1, slot],
        device_id=peer,
        device_id_type=MESH,
    )


def send(src, dst, sems, slot, peer):
    copy = remote(src, dst, sems, slot, peer)
    copy.start()
    return copy


def gather_slots(dims):
    nz, ny, nc = dims
    entries = 2 * (nz - 1) + 1
    return 2 * (nz - 1) + entries * (ny - 1) + entries * ny * (nc - 1)


def gather(at, own, full, sems, visit=lambda unit, ref: None):
    nz, ny, nc = at.dims
    entries = [(0, 0)] + [(h, way) for h in range(1, nz) for way in (1, -1)]
    hops = {e: n for n, e in enumerate(entries[1:])}
    slot = len(hops)
    sides, cores = {}, {}
    for e in entries:
        for j in range(1, ny):
            sides[e, j] = slot
            slot += 1
    for e in entries:
        for j in range(ny):
            for i in range(1, nc):
                cores[e, j, i] = slot
                slot += 1

    def source(e, j=0):
        h, way = e
        z = at.z - way * h
        if h == 0 and j == 0:
            return own, at.unit(z)
        u = at.unit(z, -j)
        return full.at[u], u

    def guarded(e, body):
        if e[0] == 0:
            body()
        else:
            pl.when(at.has(at.z - e[1] * e[0]))(body)

    def hop(e):
        h, way = e
        src, u = source((h - 1, way))
        return remote(src, full.at[u], sems, hops[e], at.peer(k=way))

    def side(e, j):
        src, u = source(e)
        return remote(src, full.at[u], sems, sides[e, j], at.peer(j=j))

    def core(e, j, i):
        src, u = source(e, j)
        return remote(src, full.at[u], sems, cores[e, j, i], at.peer(i=i))

    def pass_on(e):
        h, way = e
        for onward in (1, -1) if h == 0 else (way,):
            if h + 1 < nz:

                @pl.when(at.has(at.z + onward))
                def _():
                    hop((h + 1, onward)).start()

        for j in range(1, ny):
            side(e, j).start()
        for i in range(1, nc):
            core(e, 0, i).start()
        src, u = source(e)
        visit(u, src)

    def from_side(e):
        for j in range(1, ny):
            side(e, j).wait_recv()
            for i in range(1, nc):
                core(e, j, i).start()
            src, u = source(e, j)
            visit(u, src)

    def from_core(e):
        for j in range(ny):
            for i in range(1, nc):
                core(e, j, i).wait_recv()
                u = at.unit(at.z - e[1] * e[0], -j, -i)
                visit(u, full.at[u])

    pass_on((0, 0))
    for e in entries[1:]:

        def arrived(e=e):
            hop(e).wait_recv()
            pass_on(e)

        guarded(e, arrived)
    for e in entries:
        guarded(e, functools.partial(from_side, e))
    for e in entries:
        guarded(e, functools.partial(from_core, e))

    def drain(e):
        for j in range(1, ny):
            side(e, j).wait_send()
        for j in range(ny):
            for i in range(1, nc):
                core(e, j, i).wait_send()

    for e in entries:
        guarded(e, functools.partial(drain, e))
    for h, way in entries[1:]:

        @pl.when(jnp.logical_and(at.has(at.z + way), at.has(at.z - way * (h - 1))))
        def _():
            hop((h, way)).wait_send()


def project_kernel(
    dims, tensor, in_ref, basis_ref, out_ref, back,
    rows_in, own, full, acc, sent, got, sems, gather_sems, local,
):
    at = Place(dims, tensor)
    dp = math.prod(dims)
    per = dp // tensor
    swaps = at.t != at.d // per
    partner = (at.t * per + at.d % per, at.d // per)
    load = pltpu.make_async_copy(in_ref, rows_in, local.at[0])
    mine = pltpu.make_async_copy(basis_ref, own, local.at[1])
    mine_back = pltpu.make_async_copy(basis_ref, back.at[at.t], local.at[2])
    greet(at.peers(), (swaps, partner))
    swap = remote(basis_ref, own, sems, 0, partner)

    @pl.when(swaps)
    def _():
        swap.start()

    @pl.when(jnp.logical_not(swaps))
    def _():
        mine.start()

    load.start()
    mine_back.start()
    backs = [
        send(basis_ref, back.at[at.t], sems, s, at.peer(s=s)) for s in range(1, tensor)
    ]
    acc[...] = jnp.zeros_like(acc)
    load.wait()

    @pl.when(swaps)
    def _():
        swap.wait()

    @pl.when(jnp.logical_not(swaps))
    def _():
        mine.wait()

    depth, width = own.shape

    def visit(unit, ref):
        columns = pl.ds(pl.multiple_of((unit % per) * depth, depth), depth)
        acc[unit // per] += jnp.dot(
            rows_in[:, columns], ref[...], preferred_element_type=jnp.float32
        )

    gather(at, own, full, gather_sems, visit)

    copies = []
    for h in range(tensor):
        sent[h] = acc[h].astype(jnp.bfloat16)
        for s in range(1, tensor):
            copies.append(
                send(
                    sent.at[h],
                    got.at[s - 1, h],
                    sems,
                    tensor + h * (tensor - 1) + s - 1,
                    at.peer(s=s),
                )
            )
    for h in range(tensor):
        total = acc[h]
        for s in range(1, tensor):
            copies[h * (tensor - 1) + s - 1].wait_recv()
            total = total + got[s - 1, h].astype(jnp.float32)
        out_ref[:, h * width : (h + 1) * width] = total.astype(jnp.bfloat16)
    for copy in copies:
        copy.wait_send()
    for copy in backs:
        copy.wait()
    mine_back.wait()


def project(inputs, basis, dims, tensor):
    dp = math.prod(dims)
    tokens = inputs.shape[0]
    depth, width = basis.shape
    bf16 = jnp.bfloat16
    others = max(tensor - 1, 1)
    return pl.pallas_call(
        functools.partial(project_kernel, dims, tensor),
        out_shape=(
            jax.ShapeDtypeStruct((tokens, width * tensor), bf16),
            jax.ShapeDtypeStruct((tensor, depth, width), bf16),
        ),
        in_specs=[ANY, VMEM],
        out_specs=(VMEM, ANY),
        scratch_shapes=[
            pltpu.VMEM(inputs.shape, bf16),
            pltpu.VMEM((depth, width), bf16),
            pltpu.VMEM((dp, depth, width), bf16),
            pltpu.VMEM((tensor, tokens, width), jnp.float32),
            pltpu.VMEM((tensor, tokens, width), bf16),
            pltpu.VMEM((others, tensor, tokens, width), bf16),
            pltpu.SemaphoreType.DMA((2, tensor + tensor * others)),
            pltpu.SemaphoreType.DMA((2, max(gather_slots(dims), 1))),
            pltpu.SemaphoreType.DMA((3,)),
        ],
        compiler_params=pltpu.CompilerParams(collective_id=0, has_side_effects=True),
        name="project",
    )(inputs, basis)


def step_kernel(
    dims, tensor, bound_norm, part, m_ref, v_ref,
    first_ref, second_ref, full,
    r1, r2, r3, s1, s2, keep, upd, norm, sems, gather_sems, norm_sems, local,
):
    at = Place(dims, tensor)
    nz, ny, nc = dims
    f32 = jnp.float32
    greet(at.peers())

    entries = [(h, way) for h in range(nz - 1, 0, -1) for way in (1, -1)] + [(0, 0)]
    index = {e: n for n, e in enumerate(entries)}
    count = len(entries)

    def guarded(e, body):
        if e[0] == 0:
            body()
        else:
            pl.when(at.has(at.z + e[1] * e[0]))(body)

    def over_core(e, j, i):
        n = index[e]
        src = part.at[at.unit(at.z + e[1] * e[0], j, i)]
        slot = (n * ny + j) * (nc - 1) + i - 1
        return remote(src, r1.at[n, j, i - 1], sems, slot, at.peer(i=i))

    side_base = count * ny * (nc - 1)

    def over_side(e, j):
        n = index[e]
        slot = side_base + n * (ny - 1) + j - 1
        return remote(s1.at[n, j - 1], r2.at[n, j - 1], sems, slot, at.peer(j=j))

    line_base = side_base + count * (ny - 1)

    def over_line(h, way):
        line = 0 if way == 1 else 1
        slot = line_base + (h - 1) * 2 + line
        n = index[h, way]
        return remote(s2.at[n], r3.at[line, h - 1], sems, slot, at.peer(k=way))

    def start_cores(e):
        for j in [*range(1, ny), 0]:
            for i in range(1, nc):
                over_core(e, j, i).start()

    def core_sum(e, j):
        n = index[e]
        total = part[at.unit(at.z + e[1] * e[0], j)].astype(f32)
        for i in range(1, nc):
            over_core(e, j, i).wait_recv()
            total = total + r1[n, j, i - 1].astype(f32)
        return total

    def start_sides(e):
        n = index[e]
        for j in range(1, ny):
            s1[n, j - 1] = core_sum(e, j).astype(jnp.bfloat16)
            over_side(e, j).start()
        keep[n] = core_sum(e, 0)

    def arrive(e, way):
        line = 0 if way == 1 else 1
        over_line(e[0] + 1, way).wait_recv()
        keep[index[e]] += r3[line, e[0]].astype(f32)

    def start_line(e):
        n = index[e]
        for j in range(1, ny):
            over_side(e, j).wait_recv()
            keep[n] += r2[n, j - 1].astype(f32)
        for way in (1, -1) if e[0] == 0 else (e[1],):
            if e[0] + 1 < nz:
                pl.when(at.has(at.z - way))(functools.partial(arrive, e, way))
        if e[0]:
            s2[n] = keep[n].astype(jnp.bfloat16)
            over_line(*e).start()

    for stage in (start_cores, start_sides, start_line):
        for e in entries:
            guarded(e, functools.partial(stage, e))
    last = index[0, 0]
    total = keep[last]

    lanes = norm.shape[-1]
    columns = total.shape[1]
    squares = jnp.sum(total * total, axis=0, keepdims=True)
    folded = squares[:, :lanes]
    for a in range(1, columns // lanes):
        folded = folded + squares[:, a * lanes : (a + 1) * lanes]
    tally = jnp.broadcast_to(folded, (8, lanes))
    norm_copies, place = [], 0
    for number, axis in ((nc, "i"), (ny, "j"), (tensor, "s"), (nz, "k")):
        if number == 1:
            continue
        base = place
        norm[base] = tally
        copies = []
        for step in range(1, number):
            copies.append(
                send(norm.at[base], norm.at[base + step], norm_sems, base + step, at.peer(**{axis: step}))
            )
        for step in range(1, number):
            copies[step - 1].wait_recv()
            tally = tally + norm[base + step]
        norm_copies += copies
        place += number
    square = jnp.sum(tally[0:1, :], axis=1, keepdims=True)

    factor = jnp.minimum(1.0, bound_norm / (jnp.sqrt(square) + 1e-06))
    clipped = keep[last] * factor
    first = beta_one * m_ref[...] + (1.0 - beta_one) * clipped
    second = beta_two * v_ref[...] + (1.0 - beta_two) * clipped * clipped
    first_ref[...] = first
    second_ref[...] = second
    upd[...] = (first / corr_one / (jnp.sqrt(second / corr_two) + adam_eps)).astype(jnp.bfloat16)

    mine = pltpu.make_async_copy(upd, full.at[at.unit(at.z)], local)
    mine.start()
    gather(at, upd, full, gather_sems)
    mine.wait()

    def drain(e):
        for j in range(ny):
            for i in range(1, nc):
                over_core(e, j, i).wait_send()
            if j:
                over_side(e, j).wait_send()
        if e[0]:
            over_line(*e).wait_send()

    for e in entries:
        guarded(e, functools.partial(drain, e))
    for copy in norm_copies:
        copy.wait_send()


def reduce_step(part, first_moment, second_moment, dims, tensor, bound_norm):
    dp, rows, columns = part.shape
    nz, ny, nc = dims
    bf16, f32 = jnp.bfloat16, jnp.float32
    count = 2 * (nz - 1) + 1
    sends = count * (ny * (nc - 1) + ny - 1) + 2 * (nz - 1)
    tallies = sum(n for n in (nz, ny, nc, tensor) if n > 1)
    at_least = lambda n: max(n, 1)
    return pl.pallas_call(
        functools.partial(step_kernel, dims, tensor, bound_norm),
        out_shape=(
            jax.ShapeDtypeStruct((rows, columns), f32),
            jax.ShapeDtypeStruct((rows, columns), f32),
            jax.ShapeDtypeStruct((dp, rows, columns), bf16),
        ),
        in_specs=[VMEM, VMEM, VMEM],
        out_specs=(VMEM, VMEM, ANY),
        scratch_shapes=[
            pltpu.VMEM((count, ny, at_least(nc - 1), rows, columns), bf16),
            pltpu.VMEM((count, at_least(ny - 1), rows, columns), bf16),
            pltpu.VMEM((2, at_least(nz - 1), rows, columns), bf16),
            pltpu.VMEM((count, at_least(ny - 1), rows, columns), bf16),
            pltpu.VMEM((count, rows, columns), bf16),
            pltpu.VMEM((count, rows, columns), f32),
            pltpu.VMEM((rows, columns), bf16),
            pltpu.VMEM((at_least(tallies), 8, 128), f32),
            pltpu.SemaphoreType.DMA((2, at_least(sends))),
            pltpu.SemaphoreType.DMA((2, at_least(gather_slots(dims)))),
            pltpu.SemaphoreType.DMA((2, at_least(tallies))),
            pltpu.SemaphoreType.DMA,
        ],
        compiler_params=pltpu.CompilerParams(collective_id=1, has_side_effects=True),
        name="reduce_step",
    )(part, first_moment, second_moment)


def apply_kernel(basis_ref, update_ref, weight_ref, out_ref):
    tensor, _, width = basis_ref.shape
    delta = None
    for s in range(tensor):
        one = jnp.dot(
            basis_ref[s],
            update_ref[s * width : (s + 1) * width, :],
            preferred_element_type=jnp.float32,
        )
        delta = one if delta is None else delta + one
    kept = decay_keep * weight_ref[...].astype(jnp.float32)
    out_ref[...] = (kept - step_size * delta).astype(jnp.bfloat16)


def apply_update(basis, update, weight):
    rows, columns = weight.shape
    rank = update.shape[0]
    blocks = columns // 128
    tile = 128 * max(n for n in range(1, 9) if blocks % n == 0)
    return pl.pallas_call(
        apply_kernel,
        out_shape=jax.ShapeDtypeStruct(weight.shape, weight.dtype),
        grid=(columns // tile,),
        in_specs=[
            pl.BlockSpec(basis.shape, lambda n: (0, 0, 0)),
            pl.BlockSpec((rank, tile), lambda n: (0, n)),
            pl.BlockSpec((rows, tile), lambda n: (0, n)),
        ],
        out_specs=pl.BlockSpec((rows, tile), lambda n: (0, n)),
        name="apply_update",
    )(basis, update, weight)


def on_device(dp, tensor, inputs, out_grads, basis, weight, first_moment, second_moment):
    dims = factors(dp)
    projected, back = project(inputs, basis, dims, tensor)
    part = lax.dot_general(
        projected, out_grads, (((0,), (0,)), ((), ())), preferred_element_type=jnp.float32
    ).astype(jnp.bfloat16)
    rank, columns = part.shape
    bound_norm = math.sqrt(rank * columns * tensor)
    first, second, update = reduce_step(
        part.reshape(dp, rank // dp, columns), first_moment, second_moment, dims, tensor, bound_norm
    )
    new_weight = apply_update(back, update.reshape(rank, columns), weight)
    return (new_weight, first, second)


def solution(mesh):
    placed = P("dp", "tensor")
    return jax.shard_map(
        functools.partial(on_device, mesh.shape["dp"], mesh.shape["tensor"]),
        mesh=mesh,
        in_specs=(placed,) * 6,
        out_specs=(placed,) * 3,
        check_vma=False,
    )
```

time: 212 us -> 175 us (0.83)
  Pallas kernels: 197 us -> 162 us
    pallas_call x2 -> x1, Pallas kernels: 83.3 us -> 61.3 us  [project(): pl.pallas_call(functools.partial(project_kernel, dims, tensor), out_shape...]
    pallas_call x1, Pallas kernels: 101 us -> 88.4 us  [reduce_step(): pl.pallas_call(functools.partial(step_kernel, dims, tensor, bound_norm),...]
  transfers between devices with their start and end apart: 1 -> 0, of which waited for: 0 -> 0; matrix products, arithmetic and copies ran while one was open for 0% -> 0% of each run, Pallas kernels for 0% -> 0%
where the time goes in v2:
time: 175 us
  Pallas kernels  162 us (93%)
  matrix products  10.3 us (6%)
    pallas_call x1, Pallas kernels, reduce_step(): pl.pallas_call(functools.partial(step_kernel, dims, tensor, bound_norm),...  88.4 us
    pallas_call x1, Pallas kernels, project(): pl.pallas_call(functools.partial(project_kernel, dims, tensor), out_shape...  61.3 us
    pallas_call x1, Pallas kernels, apply_update(): pl.pallas_call(apply_kernel, out_shape=jax.ShapeDtypeStruct(weight.shape,...  12.3 us
    dot_general x1, matrix products, on_device(): lax.dot_general(projected, out_grads, (((0,), (0,)), ((), ())), preferred...  10.3 us

profile of v2, /device:TPU:0, one launch (start us, length us, event | category | flops | bytes accessed | tf_op | source)
XLA Modules:
  0.0 174.6 jit_solution(14067067851555505548)
XLA Ops:
  0.6 61.3 %project.1 = (bf16[576,512]{1,0:T(8,128)(2,1)}, bf16[2,512,256]{2,1,0:T(8,128)(2,1)}) custom-call(bf16[576,4096]{1,0:T(8,128)(2,1)} %in_ref.1, bf16[512,256]{1,0:T(8,128)(2,1)} %basis_ref.1), custom_call_target="tpu_custom_call" | custom-call | tf_op jit(solution)/shard_map/project/pallas_call | solution.py:287
  61.9 10.3 %convolution_convert_fusion = bf16[512,5632]{1,0:T(8,128)(2,1)} fusion(bf16[576,512]{1,0:T(8,128)(2,1)} %get-tuple-element.9, bf16[576,5632]{1,0:T(8,128)(2,1)} %param.7), kind=kOutput, calls=%fused_computation | convolution fusion | flops 3324772352 | bytes 12845056 | tf_op jit(solution)/shard_map/dot_general | solution.py:520
  72.2 88.4 %reduce_step.1 = (f32[32,5632]{1,0:T(8,128)}, f32[32,5632]{1,0:T(8,128)}, bf16[16,32,5632]{2,1,0:T(8,128)(2,1)}) custom-call(bf16[16,32,5632]{2,1,0:T(8,128)(2,1)} %bitcast.5, f32[32,5632]{1,0:T(8,128)} %m_ref.1, f32[32,5632]{1,0:T(8,128)} %v_ref.1), custom_call_target="tpu_custom_call" | custom-call | tf_op jit(solution)/shard_map/reduce_step/pallas_call | solution.py:456
  160.6 0.0 copy-start.1
  160.6 0.0 copy-start
  160.6 12.3 %apply_update.1 = bf16[512,5632]{1,0:T(8,128)(2,1)} custom-call(bf16[2,512,256]{2,1,0:T(8,128)(2,1)} %get-tuple-element.8.basis_ref, bf16[512,5632]{1,0:T(8,128)(2,1)} %bitcast.4, bf16[512,5632]{1,0:T(8,128)(2,1)} %weight_ref.1), custom_call_target="tpu_custom_call" | custom-call | tf_op jit(solution)/shard_map/apply_update/pallas_call | solution.py:503
  172.9 0.0 copy-done.1
  172.9 0.9 copy.11
  173.8 0.0 copy-done
  173.8 0.9 copy.12
Async XLA Ops:
  160.6 12.3 %copy-start.1 = (f32[32,5632]{1,0:T(8,128)S(1)}, f32[32,5632]{1,0:T(8,128)}, u32[]{:S(2)}) copy-start(f32[32,5632]{1,0:T(8,128)} %get-tuple-element.17) | copy-start | bytes 2162692
  160.6 13.1 %copy-start = (f32[32,5632]{1,0:T(8,128)S(1)}, f32[32,5632]{1,0:T(8,128)}, u32[]{:S(2)}) copy-start(f32[32,5632]{1,0:T(8,128)} %get-tuple-element.18) | copy-start | bytes 2162692
